TPU v7x, 32 devices: a whole 2x2x4 slice. The times are simulated.
32 devices in a mesh: mem: 4 (over x, core), lat: 8 (over z, y).
Axes of the slice: x: 2, y: 2, z: 4, core: 2. Of those that a mesh axis runs over, the one named last changes fastest.
Arguments:
- ensemble: float32 [256, 16, 512], P('mem', 'lat'), may hold values from -6 to 6
- diffusivity: float32 [16, 512], P('lat'), may hold values from 0.02 to 0.2
- north_wind: float32 [16, 512], P('lat'), may hold values from -0.25 to 0.25
- observed_blocks: int32 [8, 4, 4], P('lat'), may hold values from 0 to 7
- eastern_average_flags: int32 [8, 4, 512], P('lat'), may hold values 0 or 1
- observed_values: float32 [8, 4, 512], P('lat', 'mem'), may hold values from -6 to 6
- observed_error: float32 [8, 4, 512], P('lat', 'mem'), may hold values from 0.5 to 4
Outputs:
- analysis: float32 [256, 16, 512], P('mem', 'lat')
Inputs may be any that keep to these rules, and one draw needn't show every extreme that they name: `observed_blocks`: block i covers a band's flattened cells i * 128 to (i + 1) * 128 - 1; blocks may repeat.
All inputs are finite; a program needn't handle non-finite values. No bound on the sum of `eastern_average_flags` on one device may be relied on, other than what follows from the above.
Results may differ from a plain program's by a relative error of at most 0.0003.
Values sent between devices are 32-bit elements; how exact they have to be, the bound alone decides.
No kernel may reach another device: no remote copies, remote signals or barrier semaphores. Data moves between devices by JAX's collectives and lax.ppermute only.
A program may use at most 64 MiB of HBM per device.

v0:
```python
import jax
import jax.numpy as jnp
from jax import lax
from jax.sharding import PartitionSpec as P

OBS = 512
BLOCK = 128
NEWTON = 4
ADVECTION = 0.1
HIGHEST = lax.Precision.HIGHEST


def with_halo(block, sides, width):
    for axis, dim in sides:
        count = lax.axis_size(axis)
        forward = [(i, i + 1) for i in range(count - 1)]
        backward = [(target, source) for source, target in forward]
        low = lax.ppermute(
            lax.slice_in_dim(block, block.shape[dim] - width, None, axis=dim), axis, forward
        )
        high = lax.ppermute(lax.slice_in_dim(block, 0, width, axis=dim), axis, backward)
        block = jnp.concatenate([low, block, high], axis=dim)
    return block


def advance(padded, diffusivity, north_wind):
    centre = padded[:, 1:-1, :]
    northern = padded[:, :-2, :]
    equatorward_side = padded[:, 2:, :]
    eastern = jnp.roll(centre, -1, axis=2)
    western_neighbour = jnp.roll(centre, 1, axis=2)
    return (
        centre
        - ADVECTION * centre * (eastern - western_neighbour)
        - north_wind * (equatorward_side - northern)
        + diffusivity * (eastern + western_neighbour + northern + equatorward_side - 4.0 * centre)
    )


def contract_first(left, right):
    return lax.dot_general(
        left, right, (((0,), (0,)), ((), ())), precision=HIGHEST, preferred_element_type=jnp.float32
    )


def patch_gain(cell_values, seen_values, values, errors):
    sample_states = cell_values.shape[0]
    cell_offset = cell_values - jnp.mean(cell_values, axis=0)
    seen_mean = jnp.mean(seen_values, axis=0)
    seen_offset = seen_values - seen_mean
    covariance = contract_first(seen_offset, seen_offset) / (sample_states - 1.0) + jnp.diag(errors)
    row_scale = jnp.sum(jnp.abs(covariance), axis=1)
    inverse = jnp.diag(1.0 / row_scale)
    for sweep in range(NEWTON):
        product = jnp.dot(
            covariance, inverse, precision=HIGHEST, preferred_element_type=jnp.float32
        )
        inverse = 2.0 * inverse - jnp.dot(
            inverse, product, precision=HIGHEST, preferred_element_type=jnp.float32
        )
    cross_cov = contract_first(cell_offset, seen_offset) / (sample_states - 1.0)
    gain = jnp.dot(cross_cov, inverse, precision=HIGHEST, preferred_element_type=jnp.float32)
    innovation = values - seen_mean
    return (gain, innovation, seen_mean)


def body(
    ensemble,
    diffusivity,
    north_wind,
    observed_blocks,
    eastern_average_flags,
    observed_values,
    observed_error,
):
    local_members, row_count, meridian_total = ensemble.shape
    patch_count = lax.axis_size("mem")
    cell_count = row_count * meridian_total // patch_count
    coefficients = jnp.stack([diffusivity, north_wind])
    coef_rims = with_halo(coefficients, (("lat", 1),), 1)
    widened = with_halo(ensemble, (("lat", 1),), 2)
    variable_layers = advance(advance(widened, coef_rims[0], coef_rims[1]), diffusivity, north_wind)
    block_tiles = variable_layers.reshape(local_members, row_count * meridian_total // BLOCK, BLOCK)
    east_tiles = jnp.roll(variable_layers, -1, axis=2).reshape(
        local_members, row_count * meridian_total // BLOCK, BLOCK
    )
    chosen = observed_blocks[0].reshape(-1)
    direct = jnp.take(block_tiles, chosen, axis=1).reshape(local_members, patch_count, OBS)
    shifted = jnp.take(east_tiles, chosen, axis=1).reshape(local_members, patch_count, OBS)
    observed = jnp.where(eastern_average_flags[0][None] == 1, 0.5 * (direct + shifted), direct)
    owned = variable_layers.reshape(local_members, patch_count, cell_count)
    cell_values, seen_values = (
        lax.all_to_all(owned, "mem", split_axis=1, concat_axis=0, tiled=True),
        lax.all_to_all(observed, "mem", split_axis=1, concat_axis=0, tiled=True),
    )
    cell_values = cell_values[:, 0, :]
    seen_values = seen_values[:, 0, :]
    gain, innovation, seen_mean = patch_gain(
        cell_values, seen_values, observed_values[0, 0], observed_error[0, 0]
    )
    weights = innovation[None, :] - 0.5 * (seen_values - seen_mean[None, :])
    update = lax.dot_general(
        weights,
        gain,
        (((1,), (1,)), ((), ())),
        precision=HIGHEST,
        preferred_element_type=jnp.float32,
    )
    analysed = (cell_values + update)[:, None, :]
    returned = lax.all_to_all(analysed, "mem", split_axis=0, concat_axis=1, tiled=True)
    return returned.reshape(local_members, row_count, meridian_total)


def solution(mesh):
    return jax.shard_map(
        body,
        mesh=mesh,
        in_specs=(
            P("mem", "lat", None),
            P("lat", None),
            P("lat", None),
            P("lat", None, None),
            P("lat", None, None),
            P("lat", "mem", None),
            P("lat", "mem", None),
        ),
        out_specs=P("mem", "lat", None),
        check_vma=False,
    )
```

profile of v0, /device:TPU:0, one launch (start us, length us, event | category | flops | bytes accessed | tf_op | source)
XLA Modules:
  0.0 85.1 jit_solution(7209250416968997480)
XLA Ops:
  0.0 4.9 %collective-permute-start = (f32[64,2,512]{2,1,0:T(2,128)}, f32[64,2,512]{2,1,0:T(2,128)S(1)}, u32[]{:S(2)}, u32[]{:S(2)}) collective-permute-start(f32[64,2,512]{2,1,0:T(2,128)} %param.9), channel_id=1, source_target_pairs={{0,1},{1,2},{2,3},{3,4},{4,5},{5,6},{6,7},{8,9},{9,10},{10,11},{11... | collective-permute-start | bytes 786440 | tf_op jit(solution)/shard_map/ppermute | solution.py:18
  4.9 1.3 %collective-permute-start.1 = (f32[64,2,512]{2,1,0:T(2,128)}, f32[64,2,512]{2,1,0:T(2,128)S(1)}, u32[]{:S(2)}, u32[]{:S(2)}) collective-permute-start(f32[64,2,512]{2,1,0:T(2,128)} %param.9), channel_id=1, source_target_pairs={{1,0},{2,1},{3,2},{4,3},{5,4},{6,5},{7,6},{9,8},{10,9},{11,10},{12... | collective-permute-start | bytes 786440 | tf_op jit(solution)/shard_map/ppermute | solution.py:21
  6.2 0.8 fusion.25
  7.0 4.5 %collective-permute-start.2 = (f32[2,1,512]{2,1,0:T(1,128)S(1)}, f32[2,1,512]{2,1,0:T(1,128)S(1)}, u32[]{:S(2)}, u32[]{:S(2)}) collective-permute-start(f32[2,1,512]{2,1,0:T(1,128)S(1)} %get-tuple-element.14), channel_id=1, source_target_pairs={{0,1},{1,2},{2,3},{3,4},{4,5},{5,6},{6,7},{8,9},{9,10},{10,11},{11... | collective-permute-start | bytes 12296 | tf_op jit(solution)/shard_map/ppermute | solution.py:18
  11.6 1.3 %collective-permute-start.3 = (f32[2,1,512]{2,1,0:T(1,128)S(1)}, f32[2,1,512]{2,1,0:T(1,128)S(1)}, u32[]{:S(2)}, u32[]{:S(2)}) collective-permute-start(f32[2,1,512]{2,1,0:T(1,128)S(1)} %get-tuple-element.15), channel_id=1, source_target_pairs={{1,0},{2,1},{3,2},{4,3},{5,4},{6,5},{7,6},{9,8},{10,9},{11,10},{12... | collective-permute-start | bytes 12296 | tf_op jit(solution)/shard_map/ppermute | solution.py:21
  13.0 3.5 %collective-permute-done.2 = f32[2,1,512]{2,1,0:T(1,128)S(1)} collective-permute-done((f32[2,1,512]{2,1,0:T(1,128)S(1)}, f32[2,1,512]{2,1,0:T(1,128)S(1)}, u32[]{:S(2)}, u32[]{:S(2)}) %collective-permute-start.2) | collective-permute-done | bytes 4128 | tf_op jit(solution)/shard_map/ppermute | solution.py:18
  16.5 1.0 %collective-permute-done.3 = f32[2,1,512]{2,1,0:T(1,128)S(1)} collective-permute-done((f32[2,1,512]{2,1,0:T(1,128)S(1)}, f32[2,1,512]{2,1,0:T(1,128)S(1)}, u32[]{:S(2)}, u32[]{:S(2)}) %collective-permute-start.3) | collective-permute-done | bytes 4128 | tf_op jit(solution)/shard_map/ppermute | solution.py:21
  17.5 1.3 %pad_maximum_fusion = f32[64,6,512]{2,1,0:T(8,128)S(1)} fusion(f32[64,2,512]{2,1,0:T(2,128)S(1)} %collective-permute-done.1, f32[64,2,512]{2,1,0:T(2,128)} %param.9, f32[64,2,512]{2,1,0:T(2,128)S(1)} %collective-permute-done), kind=kLoop, calls=%fused_computation.18 | loop fusion | flops 393216 | bytes 1572864 | tf_op jit(solution)/shard_map/concatenate | solution.py:22
  18.8 0.5 fusion.29
  19.3 0.5 copy-done
  19.8 1.3 %multiply_add_fusion = f32[64,4,512]{2,1,0:T(4,128)S(1)} fusion(f32[64,2,512]{2,1,0:T(2,128)S(1)} %copy-done, f32[64,2,512]{2,1,0:T(2,128)S(1)} %collective-permute-done, f32[64,2,512]{2,1,0:T(2,128)S(1)} %collective-permute-done.1, f32[64,4,511]{2,1,0:T(4,128)S(1)} %get-tuple-element.7, f32[64,4,511]{2,1,0:T(4,128)S(1)} %get-tuple-element.6, ...), kind=kLoop, calls=%fused_computation.42 | loop fusion | flops 2883584 | bytes 2897920 | tf_op jit(solution)/shard_map/add | solution.py:33
  21.1 0.5 fusion.30
  21.7 0.9 %multiply_add_fusion.1 = f32[64,2,512]{2,1,0:T(2,128)S(1)} fusion(f32[64,4,512]{2,1,0:T(4,128)S(1)} %multiply_add_fusion, f32[64,2,511]{2,1,0:T(2,128)S(1)} %get-tuple-element.9, f32[64,2,1]{2,1,0:T(2,128)S(1)} %get-tuple-element.11, f32[64,2,1]{2,1,0:T(2,128)S(1)} %get-tuple-element.10, f32[64,2,511]{2,1,0:T(2,128)S(1)} %get-tuple-element.8, ...), kind=kLoop, calls=%fused_computation.50 | loop fusion | flops 1048576 | bytes 1581056 | tf_op jit(solution)/shard_map/add | solution.py:33
  22.6 0.3 slice.110
  22.9 0.2 reshape.83
  23.1 0.3 reshape.82
  23.6 0.2 reshape.85
  23.9 0.6 gather_fusion.1
  24.5 0.6 gather_fusion
  25.2 0.3 copy.38
  25.6 0.2 reshape.84
  25.8 0.3 copy.40
  26.1 0.2 reshape.86
  26.3 0.8 copy.36
  27.0 3.4 %all-to-all-start = ((f32[64,4,256]{2,0,1:T(8,128)}), f32[64,4,256]{2,0,1:T(8,128)S(1)}, u32[]{:S(2)}, u32[]{:S(2)}) async-start(f32[64,4,256]{2,0,1:T(8,128)} %copy.36), calls=%async_computation | async-start | bytes 524288 | tf_op jit(solution)/shard_map/all_to_all | solution.py:93
  30.4 0.2 multiply_select_fusion
  30.6 1.0 %copy.41 = f32[64,4,512]{2,0,1:T(8,128)} copy(f32[64,4,512]{2,1,0:T(4,128)S(1)} %multiply_select_fusion) | data formatting | bytes 1048576 | tf_op jit(solution)/shard_map/jit(_where)/select_n | solution.py:90
  31.6 4.8 %all-to-all-done = f32[64,4,256]{2,0,1:T(8,128)S(1)} async-done(((f32[64,4,256]{2,0,1:T(8,128)}), f32[64,4,256]{2,0,1:T(8,128)S(1)}, u32[]{:S(2)}, u32[]{:S(2)}) %all-to-all-start) | async-done | bytes 262176 | tf_op jit(solution)/shard_map/all_to_all | solution.py:93
  36.4 3.6 %all-to-all-start.1 = ((f32[64,4,512]{2,0,1:T(8,128)}), f32[64,4,512]{2,0,1:T(8,128)S(1)}, u32[]{:S(2)}, u32[]{:S(2)}) async-start(f32[64,4,512]{2,0,1:T(8,128)} %copy.41), calls=%async_computation.1 | async-start | bytes 1048576 | tf_op jit(solution)/shard_map/all_to_all | solution.py:94
  40.1 8.5 %all-to-all-done.1 = f32[64,4,512]{2,0,1:T(8,128)S(1)} async-done(((f32[64,4,512]{2,0,1:T(8,128)}), f32[64,4,512]{2,0,1:T(8,128)S(1)}, u32[]{:S(2)}, u32[]{:S(2)}) %all-to-all-start.1) | async-done | bytes 524320 | tf_op jit(solution)/shard_map/all_to_all | solution.py:94
  48.7 0.6 copy-done.5
  49.3 0.7 copy-done.6
  50.0 1.2 %abs_reduce_fusion = (f32[512]{0:T(512)S(1)}, f32[512,512]{0,1:T(8,128)S(1)}) fusion(f32[512]{0:T(512)S(1)} %bitcast.94, f32[64,4,512]{2,0,1:T(8,128)S(1)} %all-to-all-done.1, f32[512]{0:T(512)S(1)} %get-tuple-element.17), kind=kOutput, calls=%fused_computation.19 | convolution fusion | flops 807009792 | bytes 1579008 | tf_op jit(solution)/shard_map/dot_general | solution.py:41
  51.2 3.5 %fusion.2 = f32[512,512]{1,0:T(8,128)S(1)} fusion(f32[512,512]{0,1:T(8,128)S(1)} %get-tuple-element.21, f32[512]{0:T(512)S(1)} %broadcast_divide_fusion), kind=kOutput, calls=%fused_computation.4 | convolution fusion | flops 1611137024 | bytes 2099200 | tf_op jit(solution)/shard_map/dot_general | solution.py:55
  54.7 1.9 %fusion.4 = f32[512,512]{0,1:T(8,128)S(1)} fusion(f32[512,512]{1,0:T(8,128)S(1)} %fusion.2, f32[512]{0:T(512)S(1)} %broadcast_divide_fusion), kind=kOutput, calls=%fused_computation.7 | convolution fusion | flops 1612185600 | bytes 2099200 | tf_op jit(solution)/shard_map/dot_general | solution.py:58
  56.6 3.5 %fusion.32 = f32[512,512]{1,0:T(8,128)S(1)} fusion(f32[512,512]{0,1:T(8,128)S(1)} %get-tuple-element.21, f32[512,512]{0,1:T(8,128)S(1)} %fusion.4), kind=kOutput, calls=%fused_computation.72 | convolution fusion | flops 1610612736 | bytes 3145728 | tf_op jit(solution)/shard_map/dot_general | solution.py:55
  60.1 1.9 %convolution_subtract_fusion.2 = f32[512,512]{0,1:T(8,128)S(1)} fusion(f32[512,512]{0,1:T(8,128)S(1)} %fusion.4, f32[512,512]{1,0:T(8,128)S(1)} %fusion.32), kind=kOutput, calls=%fused_computation.10 | convolution fusion | flops 1611137024 | bytes 3145728 | tf_op jit(solution)/shard_map/dot_general | solution.py:58
  62.0 3.7 %fusion.33 = f32[512,512]{1,0:T(8,128)S(1)} fusion(f32[512,512]{0,1:T(8,128)S(1)} %get-tuple-element.21, f32[512,512]{0,1:T(8,128)S(1)} %convolution_subtract_fusion.2), kind=kOutput, calls=%fused_computation.73 | convolution fusion | flops 1610612736 | bytes 3145728 | tf_op jit(solution)/shard_map/dot_general | solution.py:55
  65.7 1.9 %convolution_subtract_fusion.1 = f32[512,512]{0,1:T(8,128)S(1)} fusion(f32[512,512]{0,1:T(8,128)S(1)} %convolution_subtract_fusion.2, f32[512,512]{1,0:T(8,128)S(1)} %fusion.33), kind=kOutput, calls=%fused_computation.9 | convolution fusion | flops 1611137024 | bytes 3145728 | tf_op jit(solution)/shard_map/dot_general | solution.py:58
  67.5 3.5 %fusion.34 = f32[512,512]{1,0:T(8,128)S(1)} fusion(f32[512,512]{0,1:T(8,128)S(1)} %get-tuple-element.21, f32[512,512]{0,1:T(8,128)S(1)} %convolution_subtract_fusion.1), kind=kOutput, calls=%fused_computation.74 | convolution fusion | flops 1610612736 | bytes 3145728 | tf_op jit(solution)/shard_map/dot_general | solution.py:55
  71.0 1.9 %convolution_subtract_fusion = f32[512,512]{0,1:T(8,128)S(1)} fusion(f32[512,512]{0,1:T(8,128)S(1)} %convolution_subtract_fusion.1, f32[512,512]{1,0:T(8,128)S(1)} %fusion.34), kind=kOutput, calls=%fused_computation.8 | convolution fusion | flops 1611137024 | bytes 3145728 | tf_op jit(solution)/shard_map/dot_general | solution.py:58
  72.9 0.7 fusion.9
  73.6 1.1 %fusion.35 = f32[256,512]{1,0:T(8,128)S(1)} fusion(f32[256,512]{1,0:T(8,128)S(1)} %fusion.9, f32[512,512]{0,1:T(8,128)S(1)} %convolution_subtract_fusion), kind=kOutput, calls=%fused_computation.75 | convolution fusion | flops 805306368 | bytes 2097152 | tf_op jit(solution)/shard_map/dot_general | solution.py:62
  74.7 0.6 fusion.10
  75.4 0.3 copy.46
  75.6 8.4 %all_to_all.45 = f32[256,1,256]{2,1,0:T(1,128)S(1)} all-to-all(f32[256,1,256]{2,1,0:T(1,128)S(1)} %copy.46), channel_id=1, replica_groups=mesh['mem'=4,'lat'=8] {'mem'}, dimensions={0} | all-to-all | bytes 524288 | tf_op jit(solution)/shard_map/all_to_all | solution.py:110
  84.0 0.2 copy.47
  84.2 0.9 %reshape.89 = f32[64,2,512]{2,1,0:T(2,128)} reshape(f32[64,4,1,256]{3,1,0,2:T(4,128)S(1)} %copy.47) | data formatting | bytes 524288 | tf_op jit(solution)/shard_map/reshape | solution.py:111
  (32 shorter events, 0.9 us)
Async XLA Ops:
  0.0 17.5 %collective-permute-start = (f32[64,2,512]{2,1,0:T(2,128)}, f32[64,2,512]{2,1,0:T(2,128)S(1)}, u32[]{:S(2)}, u32[]{:S(2)}) collective-permute-start(f32[64,2,512]{2,1,0:T(2,128)} %param.9), channel_id=1, source_target_pairs={{0,1},{1,2},{2,3},{3,4},{4,5},{5,6},{6,7},{8,9},{9,10},{10,11},{11... | collective-permute-start | bytes 786440 | tf_op jit(solution)/shard_map/ppermute | solution.py:18
  4.9 12.6 %collective-permute-start.1 = (f32[64,2,512]{2,1,0:T(2,128)}, f32[64,2,512]{2,1,0:T(2,128)S(1)}, u32[]{:S(2)}, u32[]{:S(2)}) collective-permute-start(f32[64,2,512]{2,1,0:T(2,128)} %param.9), channel_id=1, source_target_pairs={{1,0},{2,1},{3,2},{4,3},{5,4},{6,5},{7,6},{9,8},{10,9},{11,10},{12... | collective-permute-start | bytes 786440 | tf_op jit(solution)/shard_map/ppermute | solution.py:21
  6.2 6.7 %copy-start.4 = (s32[1,4,4]{2,1,0:T(4,128)S(1)}, s32[1,4,4]{2,1,0:T(4,128)}, u32[]{:S(2)}) copy-start(s32[1,4,4]{2,1,0:T(4,128)} %param.12) | copy-start | bytes 196
  7.0 6.0 %copy-start.3 = (s32[1,4,512]{2,1,0:T(4,128)S(1)}, s32[1,4,512]{2,1,0:T(4,128)}, u32[]{:S(2)}) copy-start(s32[1,4,512]{2,1,0:T(4,128)} %param.13) | copy-start | bytes 24580
  7.0 9.5 %collective-permute-start.2 = (f32[2,1,512]{2,1,0:T(1,128)S(1)}, f32[2,1,512]{2,1,0:T(1,128)S(1)}, u32[]{:S(2)}, u32[]{:S(2)}) collective-permute-start(f32[2,1,512]{2,1,0:T(1,128)S(1)} %get-tuple-element.14), channel_id=1, source_target_pairs={{0,1},{1,2},{2,3},{3,4},{4,5},{5,6},{6,7},{8,9},{9,10},{10,11},{11... | collective-permute-start | bytes 12296 | tf_op jit(solution)/shard_map/ppermute | solution.py:18
  11.6 5.9 %collective-permute-start.3 = (f32[2,1,512]{2,1,0:T(1,128)S(1)}, f32[2,1,512]{2,1,0:T(1,128)S(1)}, u32[]{:S(2)}, u32[]{:S(2)}) collective-permute-start(f32[2,1,512]{2,1,0:T(1,128)S(1)} %get-tuple-element.15), channel_id=1, source_target_pairs={{1,0},{2,1},{3,2},{4,3},{5,4},{6,5},{7,6},{9,8},{10,9},{11,10},{12... | collective-permute-start | bytes 12296 | tf_op jit(solution)/shard_map/ppermute | solution.py:21
  13.0 4.5 %copy-start.2 = (f32[2,512]{1,0:T(2,128)S(1)}, f32[2,512]{1,0:T(2,128)}, u32[]{:S(2)}) copy-start(f32[2,512]{1,0:T(2,128)} %param.11) | copy-start | bytes 12292
  13.0 4.5 %copy-start.1 = (f32[2,512]{1,0:T(2,128)S(1)}, f32[2,512]{1,0:T(2,128)}, u32[]{:S(2)}) copy-start(f32[2,512]{1,0:T(2,128)} %param.10) | copy-start | bytes 12292
  18.8 1.0 %copy-start = (f32[64,2,512]{2,1,0:T(2,128)S(1)}, f32[64,2,512]{2,1,0:T(2,128)}, u32[]{:S(2)}) copy-start(f32[64,2,512]{2,1,0:T(2,128)} %param.9) | copy-start | bytes 786436
  27.0 9.4 %all-to-all-start = ((f32[64,4,256]{2,0,1:T(8,128)}), f32[64,4,256]{2,0,1:T(8,128)S(1)}, u32[]{:S(2)}, u32[]{:S(2)}) async-start(f32[64,4,256]{2,0,1:T(8,128)} %copy.36), calls=%async_computation | async-start | bytes 524288 | tf_op jit(solution)/shard_map/all_to_all | solution.py:93
  36.4 12.3 %all-to-all-start.1 = ((f32[64,4,512]{2,0,1:T(8,128)}), f32[64,4,512]{2,0,1:T(8,128)S(1)}, u32[]{:S(2)}, u32[]{:S(2)}) async-start(f32[64,4,512]{2,0,1:T(8,128)} %copy.41), calls=%async_computation.1 | async-start | bytes 1048576 | tf_op jit(solution)/shard_map/all_to_all | solution.py:94
  48.7 0.7 copy-start.5
  49.3 0.7 copy-start.6
where the time goes:
time: 85.7 us; the launch traced here: 85.1 us
  matrix products  25.2 us (29%)
  starting transfers between devices  19.1 us (22%)
  waiting for transfers between devices  17.8 us (21%)
  local copies, waits for them, and re-layouts  9.31 us (11%)
  blocking collectives  8.39 us (10%)
  other arithmetic  4.96 us (6%)
    dot_general x4, matrix products, patch_gain(): jnp.dot(covariance, inverse, precision=HIGHEST, preferred_element_type=jn...  14.1 us
    ppermute x2, starting transfers between devices, with_halo(): lax.ppermute(lax.slice_in_dim(block, block.shape[dim] - width, None, axis...  9.45 us
    all_to_all x1, waiting for transfers between devices, body(): lax.all_to_all(observed, 'mem', split_axis=1, concat_axis=0, tiled=True)  8.54 us
    all_to_all x1, blocking collectives, body(): lax.all_to_all(analysed, 'mem', split_axis=0, concat_axis=1, tiled=True)  8.39 us
    dot_general x4, matrix products, patch_gain(): jnp.dot(inverse, product, precision=HIGHEST, preferred_element_type=jnp.f...  7.55 us
    all_to_all x1, waiting for transfers between devices, body(): lax.all_to_all(owned, 'mem', split_axis=1, concat_axis=0, tiled=True)  4.83 us
    all_to_all x1, starting transfers between devices, body(): lax.all_to_all(observed, 'mem', split_axis=1, concat_axis=0, tiled=True)  3.65 us
    ppermute x2, waiting for transfers between devices, with_halo(): lax.ppermute(lax.slice_in_dim(block, block.shape[dim] - width, None, axis...  3.46 us
  transfers between devices with their start and end apart: 6, of which 4 were waited for; matrix products, arithmetic and copies ran while one was open for 2% of the time, Pallas kernels for 0%

commit v1 on v0

--- a/solution.py
+++ b/solution.py
@@ -8,6 +8,29 @@
 NEWTON = 4
 ADVECTION = 0.1
 HIGHEST = lax.Precision.HIGHEST
+
+
+def cut_along(x, dim, size):
+    before, after = (x.shape[:dim], x.shape[dim + 1 :])
+    return jnp.moveaxis(x.reshape(*before, size, -1, *after), dim, 0)
+
+
+def in_order(pieces, dim):
+    pieces = jnp.moveaxis(pieces, 0, dim)
+    lengths = pieces.shape
+    return pieces.reshape(*lengths[:dim], lengths[dim] * lengths[dim + 1], *lengths[dim + 2 :])
+
+
+def sent_to_each(x, axis, split_dim, concat_dim):
+    size, index = (lax.axis_size(axis), lax.axis_index(axis))
+    pieces = cut_along(x, split_dim, size)
+    result = pieces
+    for step in range(1, size):
+        target, source = ((index + step) % size, (index - step) % size)
+        sent = lax.dynamic_index_in_dim(pieces, target, 0)
+        other = lax.ppermute(sent, axis, [(i, (i + step) % size) for i in range(size)])
+        result = lax.dynamic_update_slice_in_dim(result, other, source, axis=0)
+    return in_order(result, concat_dim)
 
 
 def with_halo(block, sides, width):
@@ -91,7 +114,7 @@
     owned = variable_layers.reshape(local_members, patch_count, cell_count)
     cell_values, seen_values = (
         lax.all_to_all(owned, "mem", split_axis=1, concat_axis=0, tiled=True),
-        lax.all_to_all(observed, "mem", split_axis=1, concat_axis=0, tiled=True),
+        sent_to_each(observed, "mem", 1, 0),
     )
     cell_values = cell_values[:, 0, :]
     seen_values = seen_values[:, 0, :]

time: 85.7 us -> 76.6 us (0.89)
  waiting for transfers between devices: 17.8 us -> 4 us
  local copies, waits for them, and re-layouts: 9.31 us -> 12.6 us
    all_to_all x1 -> x0, waiting for transfers between devices: 8.54 us -> none  [body(): lax.all_to_all(observed, 'mem', split_axis=1, concat_axis=0, tiled=True)]
    all_to_all x1, waiting for transfers between devices: 4.83 us -> 0.01 us  [body(): lax.all_to_all(owned, 'mem', split_axis=1, concat_axis=0, tiled=True)]
    dynamic_update_slice x0 -> x4, local copies, waits for them, and re-layouts: none -> 4.11 us  [sent_to_each(): result = lax.dynamic_update_slice_in_dim(result, other, source, axis=0)]
    all_to_all x1 -> x0, starting transfers between devices: 3.65 us -> none  [body(): lax.all_to_all(observed, 'mem', split_axis=1, concat_axis=0, tiled=True)]
    ppermute x0 -> x3, starting transfers between devices: none -> 3 us  [sent_to_each(): lax.ppermute(sent, axis, [(i, (i + step) % size) for i in range(size)])]
    select_n x1 -> x0, local copies, waits for them, and re-layouts: 0.95 us -> none  [body(): jnp.where(eastern_average_flags[0][None] == 1, 0.5 * (direct + shifted),...]
    ppermute x2, starting transfers between devices: 9.45 us -> 10.4 us  [with_halo(): lax.ppermute(lax.slice_in_dim(block, block.shape[dim] - width, None, axis...]
  transfers between devices with their start and end apart: 6 -> 8, of which waited for: 4 -> 2; matrix products, arithmetic and copies ran while one was open for 2% -> 39% of each run, Pallas kernels for 0% -> 0%
where the time goes in v1:
time: 76.6 us; the launch traced here: 76.1 us
  matrix products  25.5 us (33%)
  starting transfers between devices  19.3 us (25%)
  local copies, waits for them, and re-layouts  12.6 us (16%)
  blocking collectives  9.04 us (12%)
  other arithmetic  5.11 us (7%)
  waiting for transfers between devices  4 us (5%)
    dot_general x4, matrix products, patch_gain(): jnp.dot(covariance, inverse, precision=HIGHEST, preferred_element_type=jn...  13.9 us
    ppermute x2, starting transfers between devices, with_halo(): lax.ppermute(lax.slice_in_dim(block, block.shape[dim] - width, None, axis...  10.4 us
    all_to_all x1, blocking collectives, body(): lax.all_to_all(analysed, 'mem', split_axis=0, concat_axis=1, tiled=True)  9.04 us
    dot_general x4, matrix products, patch_gain(): jnp.dot(inverse, product, precision=HIGHEST, preferred_element_type=jnp.f...  7.79 us
    dynamic_update_slice x4, local copies, waits for them, and re-layouts, sent_to_each(): result = lax.dynamic_update_slice_in_dim(result, other, source, axis=0)  4.11 us
    all_to_all x1, starting transfers between devices, body(): lax.all_to_all(owned, 'mem', split_axis=1, concat_axis=0, tiled=True)  3.41 us
    ppermute x2, waiting for transfers between devices, with_halo(): lax.ppermute(lax.slice_in_dim(block, block.shape[dim] - width, None, axis...  3.4 us
    ppermute x3, starting transfers between devices, sent_to_each(): lax.ppermute(sent, axis, [(i, (i + step) % size) for i in range(size)])  3 us
  transfers between devices with their start and end apart: 8, of which 2 were waited for; matrix products, arithmetic and copies ran while one was open for 39% of the time, Pallas kernels for 0%

profile of v1, /device:TPU:0, one launch (start us, length us, event | category | flops | bytes accessed | tf_op | source)
XLA Modules:
  0.0 76.1 jit_solution(10931681252120149754)
XLA Ops:
  0.0 1.3 %collective-permute-start.1 = (f32[64,2,512]{2,1,0:T(2,128)}, f32[64,2,512]{2,1,0:T(2,128)S(1)}, u32[]{:S(2)}, u32[]{:S(2)}) collective-permute-start(f32[64,2,512]{2,1,0:T(2,128)} %param.9), channel_id=1, source_target_pairs={{1,0},{2,1},{3,2},{4,3},{5,4},{6,5},{7,6},{9,8},{10,9},{11,10},{12... | collective-permute-start | bytes 786440 | tf_op jit(solution)/shard_map/ppermute | solution.py:44
  1.3 5.5 %collective-permute-start = (f32[64,2,512]{2,1,0:T(2,128)}, f32[64,2,512]{2,1,0:T(2,128)S(1)}, u32[]{:S(2)}, u32[]{:S(2)}) collective-permute-start(f32[64,2,512]{2,1,0:T(2,128)} %param.9), channel_id=1, source_target_pairs={{0,1},{1,2},{2,3},{3,4},{4,5},{5,6},{6,7},{8,9},{9,10},{10,11},{11... | collective-permute-start | bytes 786440 | tf_op jit(solution)/shard_map/ppermute | solution.py:41
  6.9 0.8 %fusion.23 = (f32[2,1,512]{2,1,0:T(1,128)S(1)}, f32[2,1,512]{2,1,0:T(1,128)S(1)}) fusion(f32[1,2,512]{2,1,0:T(2,128)} %bitcast.79, f32[1,2,512]{2,1,0:T(2,128)} %bitcast.81), kind=kLoop, calls=%fused_computation.59 | loop fusion | flops 2048 | bytes 16384 | tf_op jit(solution)/shard_map/stack | solution.py:102
  7.6 4.8 %collective-permute-start.2 = (f32[2,1,512]{2,1,0:T(1,128)S(1)}, f32[2,1,512]{2,1,0:T(1,128)S(1)}, u32[]{:S(2)}, u32[]{:S(2)}) collective-permute-start(f32[2,1,512]{2,1,0:T(1,128)S(1)} %get-tuple-element.17), channel_id=1, source_target_pairs={{0,1},{1,2},{2,3},{3,4},{4,5},{5,6},{6,7},{8,9},{9,10},{10,11},{11... | collective-permute-start | bytes 12296 | tf_op jit(solution)/shard_map/ppermute | solution.py:41
  12.5 1.3 %collective-permute-start.3 = (f32[2,1,512]{2,1,0:T(1,128)S(1)}, f32[2,1,512]{2,1,0:T(1,128)S(1)}, u32[]{:S(2)}, u32[]{:S(2)}) collective-permute-start(f32[2,1,512]{2,1,0:T(1,128)S(1)} %get-tuple-element.18), channel_id=1, source_target_pairs={{1,0},{2,1},{3,2},{4,3},{5,4},{6,5},{7,6},{9,8},{10,9},{11,10},{12... | collective-permute-start | bytes 12296 | tf_op jit(solution)/shard_map/ppermute | solution.py:44
  14.0 3.4 %collective-permute-done.2 = f32[2,1,512]{2,1,0:T(1,128)S(1)} collective-permute-done((f32[2,1,512]{2,1,0:T(1,128)S(1)}, f32[2,1,512]{2,1,0:T(1,128)S(1)}, u32[]{:S(2)}, u32[]{:S(2)}) %collective-permute-start.2) | collective-permute-done | bytes 4128 | tf_op jit(solution)/shard_map/ppermute | solution.py:41
  17.4 0.6 collective-permute-done.3
  18.0 1.3 %pad_maximum_fusion = f32[64,6,512]{2,1,0:T(8,128)S(1)} fusion(f32[64,2,512]{2,1,0:T(2,128)S(1)} %collective-permute-done.1, f32[64,2,512]{2,1,0:T(2,128)} %param.9, f32[64,2,512]{2,1,0:T(2,128)S(1)} %collective-permute-done), kind=kLoop, calls=%fused_computation.18 | loop fusion | flops 393216 | bytes 1572864 | tf_op jit(solution)/shard_map/concatenate | solution.py:45
  19.3 0.5 fusion.27
  19.8 0.5 copy-done
  20.3 1.3 %multiply_add_fusion = f32[64,4,512]{2,1,0:T(4,128)S(1)} fusion(f32[64,2,512]{2,1,0:T(2,128)S(1)} %copy-done, f32[64,2,512]{2,1,0:T(2,128)S(1)} %collective-permute-done, f32[64,2,512]{2,1,0:T(2,128)S(1)} %collective-permute-done.1, f32[64,4,511]{2,1,0:T(4,128)S(1)} %get-tuple-element.7, f32[64,4,511]{2,1,0:T(4,128)S(1)} %get-tuple-element.6, ...), kind=kLoop, calls=%fused_computation.40 | loop fusion | flops 2883584 | bytes 2897920 | tf_op jit(solution)/shard_map/add | solution.py:56
  21.7 0.5 fusion.28
  22.2 0.9 %multiply_add_fusion.1 = f32[64,2,512]{2,1,0:T(2,128)S(1)} fusion(f32[64,4,512]{2,1,0:T(4,128)S(1)} %multiply_add_fusion, f32[64,2,511]{2,1,0:T(2,128)S(1)} %get-tuple-element.12, f32[64,2,1]{2,1,0:T(2,128)S(1)} %get-tuple-element.14, f32[64,2,1]{2,1,0:T(2,128)S(1)} %get-tuple-element.13, f32[64,2,511]{2,1,0:T(2,128)S(1)} %get-tuple-element.11, ...), kind=kLoop, calls=%fused_computation.48 | loop fusion | flops 1048576 | bytes 1581056 | tf_op jit(solution)/shard_map/add | solution.py:56
  23.1 0.3 slice.110
  23.4 0.2 reshape.115
  23.8 0.2 reshape.117
  24.2 0.6 gather_fusion.1
  24.7 0.6 gather_fusion
  25.5 0.3 copy.40
  25.8 0.2 reshape.118
  26.0 0.3 copy.38
  26.3 0.2 reshape.116
  26.7 0.3 dynamic-slice_bitcast_fusion
  27.1 1.6 %collective-permute-start.5 = (f32[1,64,1,512]{3,0,1,2:T(1,128)S(1)}, f32[1,64,1,512]{3,0,1,2:T(1,128)S(1)}, u32[]{:S(2)}, u32[]{:S(2)}) collective-permute-start(f32[1,64,1,512]{3,0,1,2:T(1,128)S(1)} %get-tuple-element.9), channel_id=1, source_target_pairs={{0,16},{8,24},{16,0},{24,8},{1,17},{9,25},{17,1},{25,9},{2,18},{10... | collective-permute-start | bytes 393224 | tf_op jit(solution)/shard_map/ppermute | solution.py:31
  28.6 1.4 %collective-permute-start.6 = (f32[1,64,1,512]{3,0,1,2:T(1,128)S(1)}, f32[1,64,1,512]{3,0,1,2:T(1,128)S(1)}, u32[]{:S(2)}, u32[]{:S(2)}) collective-permute-start(f32[1,64,1,512]{3,0,1,2:T(1,128)S(1)} %get-tuple-element.8), channel_id=1, source_target_pairs={{0,24},{8,0},{16,8},{24,16},{1,25},{9,1},{17,9},{25,17},{2,26},{10... | collective-permute-start | bytes 393224 | tf_op jit(solution)/shard_map/ppermute | solution.py:31
  30.0 0.3 reshape.114
  30.3 0.8 copy.36
  31.0 3.4 %all-to-all-start = ((f32[64,4,256]{2,0,1:T(8,128)}), f32[64,4,256]{2,0,1:T(8,128)S(1)}, u32[]{:S(2)}, u32[]{:S(2)}) async-start(f32[64,4,256]{2,0,1:T(8,128)} %copy.36), calls=%async_computation | async-start | bytes 524288 | tf_op jit(solution)/shard_map/all_to_all | solution.py:116
  34.5 1.3 %dynamic_update_slice.9 = f32[4,64,1,512]{3,0,1,2:T(4,128)S(1)} dynamic-update-slice(f32[4,64,1,512]{3,0,1,2:T(4,128)S(1)} %bitcast.76, f32[1,64,1,512]{3,0,1,2:T(1,128)S(1)} %collective-permute-done.4, s32[]{:T(128)S(6)} %select_n.76, s32[]{:T(128)} %constant.84.clone.1, s32[]{:T(128)} %constant.84.clone.1, s32[]{:T(128)} %constant.84.clone.1) | dynamic-update-slice | bytes 262148 | tf_op jit(solution)/shard_map/dynamic_update_slice | solution.py:32
  35.7 1.3 %dynamic_update_slice.10 = f32[4,64,1,512]{3,0,1,2:T(4,128)S(1)} dynamic-update-slice(f32[4,64,1,512]{3,0,1,2:T(4,128)S(1)} %dynamic_update_slice.9, f32[1,64,1,512]{3,0,1,2:T(1,128)S(1)} %collective-permute-done.5, s32[]{:T(128)S(6)} %select_n.80, s32[]{:T(128)} %constant.84.clone.1, s32[]{:T(128)} %constant.84.clone.1, s32[]{:T(128)} %constant.84.clone.1) | dynamic-update-slice | bytes 262148 | tf_op jit(solution)/shard_map/dynamic_update_slice | solution.py:32
  37.0 1.4 %dynamic_update_slice.11 = f32[4,64,1,512]{3,0,1,2:T(4,128)S(1)} dynamic-update-slice(f32[4,64,1,512]{3,0,1,2:T(4,128)S(1)} %dynamic_update_slice.10, f32[1,64,1,512]{3,0,1,2:T(1,128)S(1)} %collective-permute-done.6, s32[]{:T(128)S(6)} %select_n.84, s32[]{:T(128)} %constant.84.clone.1, s32[]{:T(128)} %constant.84.clone.1, s32[]{:T(128)} %constant.84.clone.1) | dynamic-update-slice | bytes 262148 | tf_op jit(solution)/shard_map/dynamic_update_slice | solution.py:32
  38.8 0.6 copy-done.5
  39.4 0.6 copy-done.6
  40.0 1.3 %abs_reduce_fusion = (f32[512]{0:T(512)S(1)}, f32[512,512]{0,1:T(8,128)S(1)}) fusion(f32[512]{0:T(512)S(1)} %bitcast.84, f32[4,64,512]{2,0,1:T(4,128)S(1)} %subtract_bitcast_fusion), kind=kOutput, calls=%fused_computation.19 | convolution fusion | flops 806878720 | bytes 1576960 | tf_op jit(solution)/shard_map/dot_general | solution.py:64
  41.4 3.5 %fusion.2 = f32[512,512]{1,0:T(8,128)S(1)} fusion(f32[512,512]{0,1:T(8,128)S(1)} %get-tuple-element.24, f32[512]{0:T(512)S(1)} %broadcast_divide_fusion), kind=kOutput, calls=%fused_computation.4 | convolution fusion | flops 1611137024 | bytes 2099200 | tf_op jit(solution)/shard_map/dot_general | solution.py:78
  44.8 1.9 %fusion.4 = f32[512,512]{0,1:T(8,128)S(1)} fusion(f32[512,512]{1,0:T(8,128)S(1)} %fusion.2, f32[512]{0:T(512)S(1)} %broadcast_divide_fusion), kind=kOutput, calls=%fused_computation.7 | convolution fusion | flops 1612185600 | bytes 2099200 | tf_op jit(solution)/shard_map/dot_general | solution.py:81
  46.7 3.5 %fusion.30 = f32[512,512]{1,0:T(8,128)S(1)} fusion(f32[512,512]{0,1:T(8,128)S(1)} %get-tuple-element.24, f32[512,512]{0,1:T(8,128)S(1)} %fusion.4), kind=kOutput, calls=%fused_computation.73 | convolution fusion | flops 1610612736 | bytes 3145728 | tf_op jit(solution)/shard_map/dot_general | solution.py:78
  50.2 2.1 %convolution_subtract_fusion.2 = f32[512,512]{0,1:T(8,128)S(1)} fusion(f32[512,512]{0,1:T(8,128)S(1)} %fusion.4, f32[512,512]{1,0:T(8,128)S(1)} %fusion.30), kind=kOutput, calls=%fused_computation.10 | convolution fusion | flops 1611137024 | bytes 3145728 | tf_op jit(solution)/shard_map/dot_general | solution.py:81
  52.4 3.5 %fusion.31 = f32[512,512]{1,0:T(8,128)S(1)} fusion(f32[512,512]{0,1:T(8,128)S(1)} %get-tuple-element.24, f32[512,512]{0,1:T(8,128)S(1)} %convolution_subtract_fusion.2), kind=kOutput, calls=%fused_computation.74 | convolution fusion | flops 1610612736 | bytes 3145728 | tf_op jit(solution)/shard_map/dot_general | solution.py:78
  55.8 1.9 %convolution_subtract_fusion.1 = f32[512,512]{0,1:T(8,128)S(1)} fusion(f32[512,512]{0,1:T(8,128)S(1)} %convolution_subtract_fusion.2, f32[512,512]{1,0:T(8,128)S(1)} %fusion.31), kind=kOutput, calls=%fused_computation.9 | convolution fusion | flops 1611137024 | bytes 3145728 | tf_op jit(solution)/shard_map/dot_general | solution.py:81
  57.7 3.5 %fusion.32 = f32[512,512]{1,0:T(8,128)S(1)} fusion(f32[512,512]{0,1:T(8,128)S(1)} %get-tuple-element.24, f32[512,512]{0,1:T(8,128)S(1)} %convolution_subtract_fusion.1), kind=kOutput, calls=%fused_computation.75 | convolution fusion | flops 1610612736 | bytes 3145728 | tf_op jit(solution)/shard_map/dot_general | solution.py:78
  61.2 1.9 %convolution_subtract_fusion = f32[512,512]{0,1:T(8,128)S(1)} fusion(f32[512,512]{0,1:T(8,128)S(1)} %convolution_subtract_fusion.1, f32[512,512]{1,0:T(8,128)S(1)} %fusion.32), kind=kOutput, calls=%fused_computation.8 | convolution fusion | flops 1611137024 | bytes 3145728 | tf_op jit(solution)/shard_map/dot_general | solution.py:81
  63.3 0.8 %fusion.9 = f32[256,512]{1,0:T(8,128)S(1)} fusion(f32[4,64,512]{2,0,1:T(4,128)S(1)} %subtract_bitcast_fusion, f32[64,4,256]{2,0,1:T(8,128)S(1)} %all-to-all-done, f32[256]{0:T(256)S(1)} %broadcast_multiply_fusion.1), kind=kOutput, calls=%fused_computation.15 | convolution fusion | flops 402849792 | bytes 1311744 | tf_op jit(solution)/shard_map/dot_general | solution.py:64
  64.0 1.1 %fusion.33 = f32[256,512]{1,0:T(8,128)S(1)} fusion(f32[256,512]{1,0:T(8,128)S(1)} %fusion.9, f32[512,512]{0,1:T(8,128)S(1)} %convolution_subtract_fusion), kind=kOutput, calls=%fused_computation.76 | convolution fusion | flops 805306368 | bytes 2097152 | tf_op jit(solution)/shard_map/dot_general | solution.py:85
  65.1 0.6 fusion.10
  65.7 0.3 copy.49
  66.0 9.0 %all_to_all.30 = f32[256,1,256]{2,1,0:T(1,128)S(1)} all-to-all(f32[256,1,256]{2,1,0:T(1,128)S(1)} %copy.49), channel_id=1, replica_groups=mesh['mem'=4,'lat'=8] {'mem'}, dimensions={0} | all-to-all | bytes 524288 | tf_op jit(solution)/shard_map/all_to_all | solution.py:133
  75.2 0.9 %reshape.121 = f32[64,2,512]{2,1,0:T(2,128)} reshape(f32[64,4,1,256]{3,1,0,2:T(4,128)S(1)} %copy.50) | data formatting | bytes 524288 | tf_op jit(solution)/shard_map/reshape | solution.py:134
  (41 shorter events, 1.7 us)
Async XLA Ops:
  0.0 18.0 %collective-permute-start.1 = (f32[64,2,512]{2,1,0:T(2,128)}, f32[64,2,512]{2,1,0:T(2,128)S(1)}, u32[]{:S(2)}, u32[]{:S(2)}) collective-permute-start(f32[64,2,512]{2,1,0:T(2,128)} %param.9), channel_id=1, source_target_pairs={{1,0},{2,1},{3,2},{4,3},{5,4},{6,5},{7,6},{9,8},{10,9},{11,10},{12... | collective-permute-start | bytes 786440 | tf_op jit(solution)/shard_map/ppermute | solution.py:44
  1.3 16.7 %collective-permute-start = (f32[64,2,512]{2,1,0:T(2,128)}, f32[64,2,512]{2,1,0:T(2,128)S(1)}, u32[]{:S(2)}, u32[]{:S(2)}) collective-permute-start(f32[64,2,512]{2,1,0:T(2,128)} %param.9), channel_id=1, source_target_pairs={{0,1},{1,2},{2,3},{3,4},{4,5},{5,6},{6,7},{8,9},{9,10},{10,11},{11... | collective-permute-start | bytes 786440 | tf_op jit(solution)/shard_map/ppermute | solution.py:41
  6.8 6.9 %copy-start.4 = (s32[1,4,4]{2,1,0:T(4,128)S(1)}, s32[1,4,4]{2,1,0:T(4,128)}, u32[]{:S(2)}) copy-start(s32[1,4,4]{2,1,0:T(4,128)} %param.12) | copy-start | bytes 196
  7.6 6.2 %copy-start.3 = (s32[1,4,512]{2,1,0:T(4,128)S(1)}, s32[1,4,512]{2,1,0:T(4,128)}, u32[]{:S(2)}) copy-start(s32[1,4,512]{2,1,0:T(4,128)} %param.13) | copy-start | bytes 24580
  7.6 9.7 %collective-permute-start.2 = (f32[2,1,512]{2,1,0:T(1,128)S(1)}, f32[2,1,512]{2,1,0:T(1,128)S(1)}, u32[]{:S(2)}, u32[]{:S(2)}) collective-permute-start(f32[2,1,512]{2,1,0:T(1,128)S(1)} %get-tuple-element.17), channel_id=1, source_target_pairs={{0,1},{1,2},{2,3},{3,4},{4,5},{5,6},{6,7},{8,9},{9,10},{10,11},{11... | collective-permute-start | bytes 12296 | tf_op jit(solution)/shard_map/ppermute | solution.py:41
  12.5 5.5 %collective-permute-start.3 = (f32[2,1,512]{2,1,0:T(1,128)S(1)}, f32[2,1,512]{2,1,0:T(1,128)S(1)}, u32[]{:S(2)}, u32[]{:S(2)}) collective-permute-start(f32[2,1,512]{2,1,0:T(1,128)S(1)} %get-tuple-element.18), channel_id=1, source_target_pairs={{1,0},{2,1},{3,2},{4,3},{5,4},{6,5},{7,6},{9,8},{10,9},{11,10},{12... | collective-permute-start | bytes 12296 | tf_op jit(solution)/shard_map/ppermute | solution.py:44
  13.9 4.0 %copy-start.2 = (f32[2,512]{1,0:T(2,128)S(1)}, f32[2,512]{1,0:T(2,128)}, u32[]{:S(2)}) copy-start(f32[2,512]{1,0:T(2,128)} %param.11) | copy-start | bytes 12292
  14.0 4.0 %copy-start.1 = (f32[2,512]{1,0:T(2,128)S(1)}, f32[2,512]{1,0:T(2,128)}, u32[]{:S(2)}) copy-start(f32[2,512]{1,0:T(2,128)} %param.10) | copy-start | bytes 12292
  19.3 1.0 %copy-start = (f32[64,2,512]{2,1,0:T(2,128)S(1)}, f32[64,2,512]{2,1,0:T(2,128)}, u32[]{:S(2)}) copy-start(f32[64,2,512]{2,1,0:T(2,128)} %param.9) | copy-start | bytes 786436
  27.0 7.4 %collective-permute-start.4 = (f32[1,64,1,512]{3,0,1,2:T(1,128)S(1)}, f32[1,64,1,512]{3,0,1,2:T(1,128)S(1)}, u32[]{:S(2)}, u32[]{:S(2)}) collective-permute-start(f32[1,64,1,512]{3,0,1,2:T(1,128)S(1)} %get-tuple-element.10), channel_id=1, source_target_pairs={{0,8},{8,16},{16,24},{24,0},{1,9},{9,17},{17,25},{25,1},{2,10},{10... | collective-permute-start | bytes 393224 | tf_op jit(solution)/shard_map/ppermute | solution.py:31
  27.1 8.6 %collective-permute-start.5 = (f32[1,64,1,512]{3,0,1,2:T(1,128)S(1)}, f32[1,64,1,512]{3,0,1,2:T(1,128)S(1)}, u32[]{:S(2)}, u32[]{:S(2)}) collective-permute-start(f32[1,64,1,512]{3,0,1,2:T(1,128)S(1)} %get-tuple-element.9), channel_id=1, source_target_pairs={{0,16},{8,24},{16,0},{24,8},{1,17},{9,25},{17,1},{25,9},{2,18},{10... | collective-permute-start | bytes 393224 | tf_op jit(solution)/shard_map/ppermute | solution.py:31
  28.6 8.4 %collective-permute-start.6 = (f32[1,64,1,512]{3,0,1,2:T(1,128)S(1)}, f32[1,64,1,512]{3,0,1,2:T(1,128)S(1)}, u32[]{:S(2)}, u32[]{:S(2)}) collective-permute-start(f32[1,64,1,512]{3,0,1,2:T(1,128)S(1)} %get-tuple-element.8), channel_id=1, source_target_pairs={{0,24},{8,0},{16,8},{24,16},{1,25},{9,1},{17,9},{25,17},{2,26},{10... | collective-permute-start | bytes 393224 | tf_op jit(solution)/shard_map/ppermute | solution.py:31
  31.0 32.1 %all-to-all-start = ((f32[64,4,256]{2,0,1:T(8,128)}), f32[64,4,256]{2,0,1:T(8,128)S(1)}, u32[]{:S(2)}, u32[]{:S(2)}) async-start(f32[64,4,256]{2,0,1:T(8,128)} %copy.36), calls=%async_computation | async-start | bytes 524288 | tf_op jit(solution)/shard_map/all_to_all | solution.py:116
  38.6 0.7 copy-start.5
  39.3 0.7 copy-start.6
